TPU v7x, 32 devices: a whole 2x2x4 slice. The times are simulated.
32 devices in a mesh: rep: 8 (over y, x, core), shard: 4 (over z).
Axes of the slice: x: 2, y: 2, z: 4, core: 2. Of those that a mesh axis runs over, the one named last changes fastest.
Arguments:
- block_input: bfloat16 [2, 5120, 1024], P(None, ('rep', 'shard')), may hold values from -6 to 6
- out_cotangent: bfloat16 [2, 5120, 1024], P(None, ('rep', 'shard')), may hold values from -6 to 6
- segment_ids: int32 [2, 5120], P(None, 'rep'), may hold values from 0 to 12, as said below
- positions: int32 [2, 5120], P(None, 'rep'), may hold values from 0 to 319, as said below
- parent_ids: int32 [2, 8, 13], P(None, 'rep'), may hold values from 0 to 12, as said below
- qkv_weight: float32 [1024, 3072], P('shard'), may hold values from -0.1875 to 0.1875
- attn_weight: float32 [1024, 1024], P('shard'), may hold values from -0.75 to 0.75
- up_weight: float32 [1024, 4096], P('shard'), may hold values from -0.1875 to 0.1875
- down_weight: float32 [4096, 1024], P('shard'), may hold values from -0.09375 to 0.09375
- small_params: float32 [13312], P('shard'), as said below
- qkv_moment: float32 [1024, 3072], P('shard'), may hold values from -448 to 448
- attn_moment: float32 [1024, 1024], P('shard'), may hold values from -96 to 96
- up_moment: float32 [1024, 4096], P('shard'), may hold values from -192 to 192
- down_moment: float32 [4096, 1024], P('shard'), may hold values from -384 to 384
- small_moment: float32 [13312], P('shard'), may hold values from -320 to 320
- qkv_average: float32 [1024, 3072], P('shard'), may hold values from -0.1875 to 0.1875
- attn_average: float32 [1024, 1024], P('shard'), may hold values from -0.75 to 0.75
- up_average: float32 [1024, 4096], P('shard'), may hold values from -0.1875 to 0.1875
- down_average: float32 [4096, 1024], P('shard'), may hold values from -0.09375 to 0.09375
- small_average: float32 [13312], P('shard'), may hold values from 0.5 to 1.5
Outputs:
- block_output: bfloat16 [2, 5120, 1024], P(None, ('rep', 'shard'))
- input_grad: float32 [2, 5120, 1024], P(None, ('rep', 'shard'))
- qkv_grad: float32 [1024, 3072], P('shard')
- attn_grad: float32 [1024, 1024], P('shard')
- up_grad: float32 [1024, 4096], P('shard')
- down_grad: float32 [4096, 1024], P('shard')
- small_grad: float32 [13312], P('shard')
- qkv_state: float32 [2, 1024, 3072], P(None, 'shard')
- attn_state: float32 [2, 1024, 1024], P(None, 'shard')
- up_state: float32 [2, 1024, 4096], P(None, 'shard')
- down_state: float32 [2, 4096, 1024], P(None, 'shard')
- small_state: float32 [2, 13312], P(None, 'shard')
- qkv_momentum: float32 [1024, 3072], P('shard')
- attn_momentum: float32 [1024, 1024], P('shard')
- up_momentum: float32 [1024, 4096], P('shard')
- down_momentum: float32 [4096, 1024], P('shard')
- small_momentum: float32 [13312], P('shard')
Inputs may be any that keep to these rules, and one draw needn't show every extreme that they name: `segment_ids`: within each tree the segment numbers never fall along the tokens; the root segment has 256 tokens, every other 32. `positions`: A token's place along its path: root tokens count from 0, a child of the root from 256, a grandchild from 288, each rising by one within its segment. `parent_ids`: the root is its own parent; it has four children, each with two children of its own. `small_params`: gains (the first and third blocks of 1024) near one; biases of both signs.
All inputs are finite; a program needn't handle non-finite values.
Results may differ from a plain program's by a relative error of at most 0.018.
Values may be sent and summed in bfloat16 or wider, within the bound.
No kernel may reach another device: no remote copies, remote signals or barrier semaphores. Data moves between devices by JAX's collectives and lax.ppermute only.
A program may use at most 256 MiB of HBM per device.

v0:
```python
from functools import partial
import math

import jax
import jax.numpy as jnp
from jax import lax
from jax.sharding import PartitionSpec as P

HEAD = 64
ROT = 16


HIGHEST = lax.Precision.HIGHEST
EPSILON = 1e-05
NEGATIVE = -1e30
MOMENTUM = 0.5
AVERAGE_DECAY = 0.5
RATES = (0.045, 0.8, 0.1, 0.024, 0.4)


def for_sending(value):
    return jax.tree.map(lambda a: a.astype(jnp.bfloat16) if a.dtype == jnp.float32 else a, value)


def layer_norm(values, gain_vec, bias_vec):
    center = values - jnp.mean(values, axis=-1, keepdims=True)
    spread = lax.rsqrt(jnp.mean(center * center, axis=-1, keepdims=True) + EPSILON)
    normed = center * spread
    return (normed * gain_vec + bias_vec, normed, spread)


def norm_back(grad_out, normed, spread, gain_vec):
    scaled = grad_out * gain_vec
    return spread * (
        scaled
        - jnp.mean(scaled, axis=-1, keepdims=True)
        - normed * jnp.mean(scaled * normed, axis=-1, keepdims=True)
    )


def rotation(pos_ids):
    half_dims = ROT // 2
    frequency = 10000.0 ** (-(jnp.arange(half_dims, dtype=jnp.float32) * 2.0) / ROT)
    angles = pos_ids.astype(jnp.float32)[:, None] * frequency[None, :]
    return (jnp.cos(angles)[:, None, :], jnp.sin(angles)[:, None, :])


def rotate(tensor, cosine_table, sine_table, direction):
    half_dims = cosine_table.shape[-1]
    first_half = tensor[..., :half_dims]
    second_half = tensor[..., half_dims : 2 * half_dims]
    return jnp.concatenate(
        [
            first_half * cosine_table - direction * second_half * sine_table,
            second_half * cosine_table + direction * first_half * sine_table,
            tensor[..., 2 * half_dims :],
        ],
        axis=-1,
    )


def ancestry(seg_ids, par_ids):
    labels = jnp.arange(par_ids.shape[0], dtype=jnp.int32)
    parent_table = par_ids.astype(jnp.float32)
    own_hot = (seg_ids[:, None] == labels[None, :]).astype(jnp.float32)
    parent_tok = jnp.dot(own_hot, parent_table, precision=HIGHEST).astype(jnp.int32)
    parent_hot = (parent_tok[:, None] == labels[None, :]).astype(jnp.float32)
    grand_tok = jnp.dot(parent_hot, parent_table, precision=HIGHEST).astype(jnp.int32)
    grand_hot = (grand_tok[:, None] == labels[None, :]).astype(jnp.float32)
    return (jnp.maximum(own_hot, jnp.maximum(parent_hot, grand_hot)), own_hot)


def block_view(kv_all, geometry, block_index):
    anc_rows, pos_rows, own_all, pos_all, block_rows, score_scale = geometry
    key_all, value_all = kv_all
    first_row = block_index * block_rows
    key_block = lax.dynamic_slice_in_dim(key_all, first_row, block_rows, 0)
    value_block = lax.dynamic_slice_in_dim(value_all, first_row, block_rows, 0)
    own_block = lax.dynamic_slice_in_dim(own_all, first_row, block_rows, 0)
    pos_block = lax.dynamic_slice_in_dim(pos_all, first_row, block_rows, 0)
    reachable = jnp.dot(anc_rows, own_block.T, precision=HIGHEST) > 0.5
    visible = reachable & (pos_block[None, :] <= pos_rows[:, None])
    return (
        key_block.reshape(block_rows, -1, HEAD),
        value_block.reshape(block_rows, -1, HEAD),
        visible,
    )


def block_scores(query_rows, key_block, visible, score_scale):
    raw_scores = jnp.einsum(
        "qhd,khd->hqk", query_rows, key_block, preferred_element_type=jnp.float32
    )
    return jnp.where(visible[None], raw_scores * score_scale, NEGATIVE)


def attend(query_rows, kv_all, geometry):
    block_rows = geometry[4]
    score_scale = geometry[5]
    block_count = kv_all[0].shape[0] // block_rows
    query_count, head_count, head_size = query_rows.shape

    def first_pass(block_index, carry):
        row_top, row_total = carry
        key_block, value_block, visible = block_view(kv_all, geometry, block_index)
        masked = block_scores(query_rows, key_block, visible, score_scale)
        new_top = jnp.maximum(row_top, jnp.max(masked, axis=-1))
        row_total = row_total * jnp.exp(row_top - new_top) + jnp.sum(
            jnp.where(visible[None], jnp.exp(masked - new_top[..., None]), 0.0), axis=-1
        )
        return (new_top, row_total)

    start_top = jnp.full((head_count, query_count), NEGATIVE, jnp.float32)
    start_total = jnp.zeros((head_count, query_count), jnp.float32)
    row_top, row_total = lax.fori_loop(0, block_count, first_pass, (start_top, start_total))
    logsum = row_top + jnp.log(row_total)

    def second_pass(block_index, accumulated):
        key_block, value_block, visible = block_view(kv_all, geometry, block_index)
        masked = block_scores(query_rows, key_block, visible, score_scale)
        probability = jnp.where(visible[None], jnp.exp(masked - logsum[..., None]), 0.0).astype(
            jnp.bfloat16
        )
        return accumulated + jnp.einsum(
            "hqk,khd->qhd", probability, value_block, preferred_element_type=jnp.float32
        )

    start_heads = jnp.zeros((query_count, head_count, head_size), jnp.float32)
    return (lax.fori_loop(0, block_count, second_pass, start_heads), logsum)


def attend_back(query_rows, kv_all, geometry, logsum, grad_heads_bf, row_delta):
    block_rows = geometry[4]
    score_scale = geometry[5]
    block_count = kv_all[0].shape[0] // block_rows

    def backward_block(grad_query, block_index):
        key_block, value_block, visible = block_view(kv_all, geometry, block_index)
        masked = block_scores(query_rows, key_block, visible, score_scale)
        probability = jnp.where(visible[None], jnp.exp(masked - logsum[..., None]), 0.0)
        grad_prob = jnp.einsum(
            "qhd,khd->hqk", grad_heads_bf, value_block, preferred_element_type=jnp.float32
        )
        grad_score = (probability * (grad_prob - row_delta[..., None])).astype(jnp.bfloat16)
        grad_query = (
            grad_query
            + jnp.einsum("hqk,khd->qhd", grad_score, key_block, preferred_element_type=jnp.float32)
            * score_scale
        )
        prob_bf = probability.astype(jnp.bfloat16)
        grad_key = (
            jnp.einsum("hqk,qhd->khd", grad_score, query_rows, preferred_element_type=jnp.float32)
            * score_scale
        )
        grad_value = jnp.einsum(
            "hqk,qhd->khd", prob_bf, grad_heads_bf, preferred_element_type=jnp.float32
        )
        return (
            grad_query,
            jnp.concatenate(
                [grad_key.reshape(block_rows, -1), grad_value.reshape(block_rows, -1)], axis=1
            ),
        )

    start_query = jnp.zeros(query_rows.shape, jnp.float32)
    grad_query, grad_blocks = lax.scan(backward_block, start_query, jnp.arange(block_count))
    return (grad_query, grad_blocks.reshape(block_count * block_rows, -1))


def local(
    block_input,
    out_cotangent,
    segment_ids,
    positions,
    parent_ids,
    qkv_weight,
    attn_weight,
    up_weight,
    down_weight,
    small_params,
    qkv_moment,
    attn_moment,
    up_moment,
    down_moment,
    small_moment,
    qkv_average,
    attn_average,
    up_average,
    down_average,
    small_average,
):
    shards = lax.axis_size("shard")
    groups = lax.axis_size("rep")
    micro_count, local_rows, model_width = block_input.shape
    head_count = model_width // HEAD
    block_rows = 2 * local_rows
    row_start = lax.axis_index("shard") * local_rows
    score_scale = HEAD ** (-0.5)
    masters = (qkv_weight, attn_weight, up_weight, down_weight, small_params)
    owned_bf = tuple((master.astype(jnp.bfloat16) for master in masters))
    block_outputs = []
    input_grads = []
    grad_totals = None
    shard_sums = None
    for micro_step in range(micro_count):
        gathered = jax.tree.map(
            lambda part, own: part.astype(own.dtype),
            lax.all_gather(for_sending(owned_bf), "shard", axis=0, tiled=True),
            owned_bf,
        )
        qkv_full, attn_full, up_full, down_full, small_full = gathered
        hidden = up_full.shape[1]
        small32 = small_full.astype(jnp.float32)
        gain_one = small32[:model_width]
        bias_one = small32[model_width : 2 * model_width]
        gain_two = small32[2 * model_width : 3 * model_width]
        bias_two = small32[3 * model_width : 4 * model_width]
        qkv_bias = small32[4 * model_width : 7 * model_width]
        attn_bias = small32[7 * model_width : 8 * model_width]
        up_bias = small32[8 * model_width : 8 * model_width + hidden]
        down_bias = small32[8 * model_width + hidden :]
        anc_all, own_all = ancestry(segment_ids[micro_step], parent_ids[micro_step, 0])
        pos_all = positions[micro_step]
        anc_rows = lax.dynamic_slice_in_dim(anc_all, row_start, local_rows, 0)
        pos_rows = lax.dynamic_slice_in_dim(pos_all, row_start, local_rows, 0)
        cosine_table, sine_table = rotation(pos_rows)
        geometry = (anc_rows, pos_rows, own_all, pos_all, block_rows, score_scale)
        inputs32 = block_input[micro_step].astype(jnp.float32)
        normed_one, unit_one, spread_one = layer_norm(inputs32, gain_one, bias_one)
        normed_two, unit_two, spread_two = layer_norm(inputs32, gain_two, bias_two)
        first_bf = normed_one.astype(jnp.bfloat16)
        second_bf = normed_two.astype(jnp.bfloat16)
        qkv_lin = jnp.dot(first_bf, qkv_full, preferred_element_type=jnp.float32) + qkv_bias
        head_shape = (local_rows, head_count, HEAD)
        query_rows = rotate(
            qkv_lin[:, :model_width].reshape(head_shape), cosine_table, sine_table, 1.0
        ).astype(jnp.bfloat16)
        key_rows = (
            rotate(
                qkv_lin[:, model_width : 2 * model_width].reshape(head_shape),
                cosine_table,
                sine_table,
                1.0,
            )
            .astype(jnp.bfloat16)
            .reshape(local_rows, model_width)
        )
        value_rows = qkv_lin[:, 2 * model_width :].astype(jnp.bfloat16)
        kv_all = (
            lax.all_gather(key_rows, "shard", axis=0, tiled=True),
            lax.all_gather(value_rows, "shard", axis=0, tiled=True),
        )
        heads_f32, logsum = attend(query_rows, kv_all, geometry)
        heads_bf = heads_f32.reshape(local_rows, model_width).astype(jnp.bfloat16)
        attn_out = jnp.dot(heads_bf, attn_full, preferred_element_type=jnp.float32) + attn_bias
        up_linear = jnp.dot(second_bf, up_full, preferred_element_type=jnp.float32) + up_bias
        activated, gelu_pull = jax.vjp(partial(jax.nn.gelu, approximate=False), up_linear)
        act_bf = activated.astype(jnp.bfloat16)
        mlp_out = jnp.dot(act_bf, down_full, preferred_element_type=jnp.float32) + down_bias
        block_outputs.append((inputs32 + attn_out + mlp_out).astype(jnp.bfloat16))
        back_weights = jax.tree.map(
            lambda part, own: part.astype(own.dtype),
            lax.all_gather(for_sending(owned_bf), "shard", axis=0, tiled=True),
            owned_bf,
        )
        back_kv = (
            lax.all_gather(key_rows, "shard", axis=0, tiled=True),
            lax.all_gather(value_rows, "shard", axis=0, tiled=True),
        )
        back_qkv = back_weights[0]
        back_attn = back_weights[1]
        back_up = back_weights[2]
        back_down = back_weights[3]
        cot_bf = out_cotangent[micro_step]
        cot32 = cot_bf.astype(jnp.float32)
        grad_down = jnp.einsum("ti,to->io", act_bf, cot_bf, preferred_element_type=jnp.float32)
        grad_act = jnp.einsum("to,io->ti", cot_bf, back_down, preferred_element_type=jnp.float32)
        grad_up_lin = gelu_pull(grad_act)[0].astype(jnp.bfloat16)
        grad_up = jnp.einsum(
            "ti,to->io", second_bf, grad_up_lin, preferred_element_type=jnp.float32
        )
        grad_second = jnp.einsum(
            "to,io->ti", grad_up_lin, back_up, preferred_element_type=jnp.float32
        )
        grad_attn = jnp.einsum("ti,to->io", heads_bf, cot_bf, preferred_element_type=jnp.float32)
        grad_heads_bf = (
            jnp.einsum("to,io->ti", cot_bf, back_attn, preferred_element_type=jnp.float32)
            .astype(jnp.bfloat16)
            .reshape(head_shape)
        )
        row_delta = jnp.sum(grad_heads_bf.astype(jnp.float32) * heads_f32, axis=-1).T
        grad_query, grad_kv_all = attend_back(
            query_rows, back_kv, geometry, logsum, grad_heads_bf, row_delta
        )
        grad_kv = lax.psum_scatter(
            grad_kv_all.astype(jnp.bfloat16), "shard", scatter_dimension=0, tiled=True
        ).astype(jnp.float32)
        grad_qkv_bf = jnp.concatenate(
            [
                rotate(grad_query, cosine_table, sine_table, -1.0).reshape(local_rows, model_width),
                rotate(
                    grad_kv[:, :model_width].reshape(head_shape), cosine_table, sine_table, -1.0
                ).reshape(local_rows, model_width),
                grad_kv[:, model_width:],
            ],
            axis=1,
        ).astype(jnp.bfloat16)
        grad_qkv = jnp.einsum(
            "ti,to->io", first_bf, grad_qkv_bf, preferred_element_type=jnp.float32
        )
        grad_first = jnp.einsum(
            "to,io->ti", grad_qkv_bf, back_qkv, preferred_element_type=jnp.float32
        )
        input_grads.append(
            cot32
            + norm_back(grad_first, unit_one, spread_one, gain_one)
            + norm_back(grad_second, unit_two, spread_two, gain_two)
        )
        grad_small = jnp.concatenate(
            [
                jnp.sum(grad_first * unit_one, axis=0),
                jnp.sum(grad_first, axis=0),
                jnp.sum(grad_second * unit_two, axis=0),
                jnp.sum(grad_second, axis=0),
                jnp.sum(grad_qkv_bf.astype(jnp.float32), axis=0),
                jnp.sum(cot32, axis=0),
                jnp.sum(grad_up_lin.astype(jnp.float32), axis=0),
                jnp.sum(cot32, axis=0),
            ]
        )
        gradients = (grad_qkv, grad_attn, grad_up, grad_down, grad_small)
        if grad_totals is None:
            grad_totals = gradients
        else:
            grad_totals = tuple((summed + added for summed, added in zip(grad_totals, gradients)))
    shard_sums = jax.tree.map(
        lambda part: part.astype(jnp.float32),
        lax.psum_scatter(for_sending(grad_totals), "shard", scatter_dimension=0, tiled=True),
    )
    summed_grads = jax.tree.map(
        lambda part: part.astype(jnp.float32), lax.psum(for_sending(shard_sums), "rep")
    )
    all_tok = micro_count * local_rows * shards * groups
    moments = (qkv_moment, attn_moment, up_moment, down_moment, small_moment)
    averages = (qkv_average, attn_average, up_average, down_average, small_average)
    states = []
    new_moments = []
    for weight_index in range(5):
        gradient = summed_grads[weight_index]
        new_moment = MOMENTUM * moments[weight_index] + gradient
        rate_now = RATES[weight_index] / math.sqrt(all_tok)
        new_weight = masters[weight_index] - rate_now * (gradient + MOMENTUM * new_moment)
        new_average = AVERAGE_DECAY * averages[weight_index] + (1.0 - AVERAGE_DECAY) * new_weight
        states.append(jnp.stack([new_weight, new_average]))
        new_moments.append(new_moment)
    return (
        jnp.stack(block_outputs),
        jnp.stack(input_grads),
        summed_grads[0],
        summed_grads[1],
        summed_grads[2],
        summed_grads[3],
        summed_grads[4],
        states[0],
        states[1],
        states[2],
        states[3],
        states[4],
        new_moments[0],
        new_moments[1],
        new_moments[2],
        new_moments[3],
        new_moments[4],
    )


def solution(mesh):
    return jax.shard_map(
        local,
        mesh=mesh,
        in_specs=(
            P(None, ("rep", "shard"), None),
            P(None, ("rep", "shard"), None),
            P(None, "rep"),
            P(None, "rep"),
            P(None, "rep", None),
            P("shard", None),
            P("shard", None),
            P("shard", None),
            P("shard", None),
            P("shard"),
            P("shard", None),
            P("shard", None),
            P("shard", None),
            P("shard", None),
            P("shard"),
            P("shard", None),
            P("shard", None),
            P("shard", None),
            P("shard", None),
            P("shard"),
        ),
        out_specs=(
            P(None, ("rep", "shard"), None),
            P(None, ("rep", "shard"), None),
            P("shard", None),
            P("shard", None),
            P("shard", None),
            P("shard", None),
            P("shard"),
            P(None, "shard", None),
            P(None, "shard", None),
            P(None, "shard", None),
            P(None, "shard", None),
            P(None, "shard"),
            P("shard", None),
            P("shard", None),
            P("shard", None),
            P("shard", None),
            P("shard"),
        ),
        check_vma=False,
    )
```

profile of v0, /device:TPU:0, one launch (start us, length us, event | category | flops | bytes accessed | tf_op | source)
XLA Modules:
  0.0 1398.7 jit_solution(1853483005798808739)
XLA Ops:
  12.4 14.9 %all-gather = bf16[4,1,3328]{2,1,0:T(2,128)(2,1)S(1)} all-gather(bf16[1,1,3328]{2,1,0:T(2,128)(2,1)S(1)} %reshape.393), channel_id=1, replica_groups=mesh['rep'=8,'shard'=4] {'shard'}, dimensions={0}, use_global_device_ids=true | all-gather | bytes 33280 | tf_op jit(solution)/shard_map/all_gather | solution.py:208
  30.1 98.9 %all-gather.10.cloned.1.call-done = bf16[1024,3072]{1,0:T(8,128)(2,1)} async-done(((bf16[256,3072]{1,0:T(8,128)(2,1)}), bf16[1024,3072]{1,0:T(8,128)(2,1)}) %all-gather.10.cloned.1.call-update) | async-done | bytes 6291472 | tf_op jit(solution)/shard_map/all_gather | solution.py:208
  129.0 4.1 convolution_add_fusion.2
  143.7 4.1 convolution_add_fusion.3
  160.3 14.6 %all-gather.16.cloned.1.call-done = bf16[1024,1024]{1,0:T(8,128)(2,1)} async-done(((bf16[256,1024]{1,0:T(8,128)(2,1)}), bf16[1024,1024]{1,0:T(8,128)(2,1)}) %all-gather.16.cloned.1.call-update) | async-done | bytes 2097168 | tf_op jit(solution)/shard_map/all_gather | solution.py:208
  198.7 9.2 all-gather.24.cloned.1.call-done
  209.6 7.0 while.88
  216.7 24.3 %all-gather.22.cloned.1.call-done = bf16[640,1024]{1,0:T(8,128)(2,1)} async-done(((bf16[160,1024]{1,0:T(8,128)(2,1)}), bf16[640,1024]{1,0:T(8,128)(2,1)}) %all-gather.22.cloned.1.call-update) | async-done | bytes 1310736 | tf_op jit(solution)/shard_map/all_gather | solution.py:251
  243.4 17.6 %while.89 = (s32[]{:T(128)}, f32[160,16,64]{0,2,1:T(8,128)}, bf16[640,1024]{0,1:T(8,128)(2,1)}, f32[640,13]{0,1:T(8,128)S(1)}, f32[160,13]{0,1:T(8,128)S(1)}, /*...) while((s32[]{:T(128)}, f32[160,16,64]{0,2,1:T(8,128)}, ...), condition=%wide.region_15.16_spmd.clone, body=%wide.region_14.15_spmd.clone.sunk | while | flops 222279680 | bytes 5730001 | solution.py:129
  247.7 4.4 fusion.363
  256.3 4.7 fusion.363
  267.1 6.9 all-gather.14.cloned.1.call-done
  276.5 9.4 while.86
  285.9 21.2 %all-gather.12.cloned.1.call-done = bf16[640,1024]{1,0:T(8,128)(2,1)} async-done(((bf16[160,1024]{1,0:T(8,128)(2,1)}), bf16[640,1024]{1,0:T(8,128)(2,1)}) %all-gather.12.cloned.1.call-update) | async-done | bytes 1310736 | tf_op jit(solution)/shard_map/all_gather | solution.py:251
  308.9 17.7 %while.87 = (s32[]{:T(128)}, f32[160,16,64]{0,2,1:T(8,128)}, bf16[640,1024]{0,1:T(8,128)(2,1)S(1)}, f32[640,13]{0,1:T(8,128)S(1)}, f32[160,13]{0,1:T(8,128)S(1)}...) while((s32[]{:T(128)}, f32[160,16,64]{0,2,1:T(8,128)}, ...), condition=%wide.region_7.8_spmd.clone, body=%wide.region_6.0_spmd.clone.sunk | while | flops 222279680 | bytes 5730001 | solution.py:129
  313.3 4.3 fusion.349
  321.9 4.7 fusion.349
  334.5 28.8 %while.90 = (s32[]{:T(128)}, f32[160,16,64]{0,2,1:T(8,128)S(1)}, bf16[2,320,2048]{2,1,0:T(8,128)(2,1)}, s32[2]{0:T(128)S(1)}, bf16[640,1024]{0,1:T(8,128)(2,1)},...) while((s32[]{:T(128)}, f32[160,16,64]{0,2,1:T(8,128)S(1)}, ...), condition=%wide.region_18.19_spmd.clone, body=%wide.region_17.18_spmd.clone.sunk | while | flops 546027520 | bytes 48400268 | solution.py:166
  365.8 25.8 %while.91 = (s32[]{:T(128)}, f32[160,16,64]{0,2,1:T(8,128)S(1)}, bf16[2,320,2048]{2,1,0:T(8,128)(2,1)}, s32[2]{0:T(128)S(1)}, bf16[640,1024]{0,1:T(8,128)(2,1)},...) while((s32[]{:T(128)}, f32[160,16,64]{0,2,1:T(8,128)S(1)}, ...), condition=%wide.region_26.27_spmd.clone, body=%wide.region_25.26_spmd.clone.sunk | while | flops 546027520 | bytes 37914460 | solution.py:166
  391.7 3.8 convert_element_type.276
  395.6 3.8 convert_element_type.278
  423.9 45.7 %reduce-scatter.9.cloned.1.call-done = bf16[160,2048]{1,0:T(8,128)(2,1)} async-done(((bf16[640,2048]{1,0:T(8,128)(2,1)}), bf16[160,2048]{1,0:T(8,128)(2,1)}) %reduce-scatter.9.cloned.1.call-update) | async-done | bytes 655376 | tf_op jit(solution)/shard_map/reduce_scatter | solution.py:295
  484.7 4.9 add_convert_fusion.2
  490.3 130.6 %all-gather.18.cloned.1.call-done = bf16[1024,4096]{1,0:T(8,128)(2,1)} async-done(((bf16[256,4096]{1,0:T(8,128)(2,1)}), bf16[1024,4096]{1,0:T(8,128)(2,1)}) %all-gather.18.cloned.1.call-update) | async-done | bytes 8388624 | tf_op jit(solution)/shard_map/all_gather | solution.py:208
  621.0 11.1 multiply_convert_fusion.1
  632.1 138.7 %all-gather.20.cloned.1.call-done = bf16[4096,1024]{1,0:T(8,128)(2,1)} async-done(((bf16[1024,1024]{1,0:T(8,128)(2,1)}), bf16[4096,1024]{1,0:T(8,128)(2,1)}) %all-gather.20.cloned.1.call-update) | async-done | bytes 8388624 | tf_op jit(solution)/shard_map/all_gather | solution.py:208
  770.8 8.5 convert_reduce_fusion.1
  780.4 9.4 fusion.189
  789.8 10.6 multiply_convert_fusion
  800.4 6.2 convert_reduce_fusion
  807.7 11.8 add_convert_fusion.1
  819.6 9.1 fusion.161
  828.7 11.6 add_convert_fusion
  842.2 5.6 convolution_add_fusion.6
  848.4 5.3 convolution_add_fusion.7
  863.2 4.2 fusion.152
  868.1 60.2 %reduce-scatter.11.cloned.1.call-done = bf16[256,3072]{1,0:T(8,128)(2,1)} async-done(((bf16[1024,3072]{1,0:T(8,128)(2,1)}), bf16[256,3072]{1,0:T(8,128)(2,1)}) %reduce-scatter.11.cloned.1.call-update) | async-done | bytes 1572880 | tf_op jit(solution)/shard_map/reduce_scatter | solution.py:338
  928.3 148.1 %reduce-scatter.15.cloned.1.call-done = bf16[256,4096]{1,0:T(8,128)(2,1)} async-done(((bf16[1024,4096]{1,0:T(8,128)(2,1)}), bf16[256,4096]{1,0:T(8,128)(2,1)}) %reduce-scatter.15.cloned.1.call-update) | async-done | bytes 2097168 | tf_op jit(solution)/shard_map/reduce_scatter | solution.py:338
  1076.4 148.0 %reduce-scatter.17.cloned.1.call-done = bf16[1024,1024]{1,0:T(8,128)(2,1)} async-done(((bf16[4096,1024]{1,0:T(8,128)(2,1)}), bf16[1024,1024]{1,0:T(8,128)(2,1)}) %reduce-scatter.17.cloned.1.call-update) | async-done | bytes 2097168 | tf_op jit(solution)/shard_map/reduce_scatter | solution.py:338
  1224.5 18.4 %all-reduce = bf16[13312]{0:T(1024)(128)(2,1)S(1)} all-reduce(bf16[13312]{0:T(1024)(128)(2,1)S(1)} %add_convert_fusion.12), channel_id=8, replica_groups=mesh['rep'=8,'shard'=4] {'shard'}, use_global_device_ids=true, to_apply=%region_54.55.clone | all-reduce | flops 13312 | bytes 53248
  1243.0 13.4 psum.39
  1260.7 72.4 %all-reduce.4.cloned.1.call-done = (bf16[256,3072]{1,0:T(8,128)(2,1)}, bf16[256,1024]{1,0:T(8,128)(2,1)}, bf16[256,4096]{1,0:T(8,128)(2,1)}, bf16[1024,1024]{1,0:T(8,128)(2,1)}) async-done(((bf16[256,3072]{1,0:T(8,128)(2,1)}, bf16[256,1024]{1,0:T(8,128)(2,1)}, bf16[256,4096]{1,0:T(8,128)(2,1)}, bf16[1024,1024]{1,0:T(8,128)(2,1)}), (bf16[256,3072]{1,0:T(8,128)(2,1)}, bf16[256,1024]{1,0:T(8,128)(2,1)}, ...) | async-done | bytes 6291472 | tf_op jit(solution)/shard_map/psum | solution.py:341
  1349.1 7.7 fusion.200
  1356.8 6.8 multiply_bitcast_fusion.1
  1363.6 6.5 pad_maximum_fusion
  1370.1 7.8 fusion.201
  1377.9 7.0 multiply_bitcast_fusion
  1385.0 6.8 pad_maximum_fusion.1
  (579 shorter events, 237.6 us)
Async XLA Ops:
  7.2 121.8 %all-gather.10.cloned.1.call-start = ((), (), s32[]{:S(2)}) async-start(), calls=%async_computation.6 | async-start | bytes 7864320 | tf_op jit(solution)/shard_map/all_gather | solution.py:208
  10.6 17.8 %copy-start.14 = (bf16[2,160,1024]{2,1,0:T(8,128)(2,1)S(1)}, bf16[2,160,1024]{2,1,0:T(8,128)(2,1)}, u32[]{:S(2)}) copy-start(bf16[2,160,1024]{2,1,0:T(8,128)(2,1)} %param.32) | copy-start | bytes 1966084
  10.6 164.3 %all-gather.16.cloned.1.call-start = ((), (), s32[]{:S(2)}) async-start(), calls=%async_computation.9 | async-start | bytes 2621440 | tf_op jit(solution)/shard_map/all_gather | solution.py:208
  11.6 196.3 %all-gather.24.cloned.1.call-start = ((), (), s32[]{:S(2)}) async-start(), calls=%async_computation.13 | async-start | bytes 1638400 | tf_op jit(solution)/shard_map/all_gather | solution.py:250
  27.4 105.7 %copy-start.77 = (f32[4,1,3328]{2,1,0:T(1,128)}, f32[4,1,3328]{2,1,0:T(1,128)S(1)}, u32[]{:S(2)}) copy-start(f32[4,1,3328]{2,1,0:T(1,128)S(1)} %convert_element_type.323) | copy-start | bytes 159748
  27.4 105.6 %copy-start.114 = (f32[3072]{0:T(1024)}, f32[3072]{0:T(1024)S(1)}, u32[]{:S(2)}) copy-start(f32[3072]{0:T(1024)S(1)} %slice.232) | copy-start | bytes 36868
  28.3 108.8 %copy-start.62 = (f32[160,8]{1,0:T(8,128)}, f32[160,8]{1,0:T(8,128)S(1)}, u32[]{:S(2)}) copy-start(f32[160,8]{1,0:T(8,128)S(1)} %copy.164) | copy-start | bytes 15364
  28.6 104.5 %copy-start.94 = (f32[160]{0:T(256)}, f32[160]{0:T(256)S(1)}, u32[]{:S(2)}) copy-start(f32[160]{0:T(256)S(1)} %get-tuple-element.1606) | copy-start | bytes 1924
  28.6 115.0 %copy-start.84 = (f32[160]{0:T(256)}, f32[160]{0:T(256)S(1)}, u32[]{:S(2)}) copy-start(f32[160]{0:T(256)S(1)} %get-tuple-element.1607) | copy-start | bytes 1924
  29.4 103.6 %copy-start.96 = (f32[160]{0:T(256)}, f32[160]{0:T(256)S(1)}, u32[]{:S(2)}) copy-start(f32[160]{0:T(256)S(1)} %add_rsqrt_fusion) | copy-start | bytes 1924
  30.1 113.6 %copy-start.72 = (f32[1024]{0:T(1024)}, f32[1024]{0:T(1024)S(1)}, u32[]{:S(2)}) copy-start(f32[1024]{0:T(1024)S(1)} %get-tuple-element.1587) | copy-start | bytes 12292
  30.1 113.6 %copy-start.75 = (f32[1024]{0:T(1024)}, f32[1024]{0:T(1024)S(1)}, u32[]{:S(2)}) copy-start(f32[1024]{0:T(1024)S(1)} %get-tuple-element.1586) | copy-start | bytes 12292
  140.9 100.1 %all-gather.22.cloned.1.call-start = ((), (), s32[]{:S(2)}) async-start(), calls=%async_computation.12 | async-start | bytes 1638400 | tf_op jit(solution)/shard_map/all_gather | solution.py:251
  142.8 131.2 %all-gather.14.cloned.1.call-start = ((), (), s32[]{:S(2)}) async-start(), calls=%async_computation.8 | async-start | bytes 1638400 | tf_op jit(solution)/shard_map/all_gather | solution.py:250
  143.5 10.4 copy-start.64
  157.6 149.5 %all-gather.12.cloned.1.call-start = ((), (), s32[]{:S(2)}) async-start(), calls=%async_computation.7 | async-start | bytes 1638400 | tf_op jit(solution)/shard_map/all_gather | solution.py:251
  184.7 8.3 copy-start.31
  197.6 12.0 copy-start.104
  197.6 12.0 copy-start.120
  198.2 222.3 %reduce-scatter.7.cloned.1.call-start = ((), (), s32[]{:S(2)}) async-start(), calls=%async_computation.14 | async-start | bytes 3276800 | tf_op jit(solution)/shard_map/reduce_scatter | solution.py:295
  216.7 26.7 %copy-start.105 = (f32[160,13]{0,1:T(8,128)S(1)}, f32[160,13]{0,1:T(8,128)}, u32[]{:S(2)}) copy-start(f32[160,13]{0,1:T(8,128)} %dynamic-slice_maximum_fusion) | copy-start | bytes 24964
  261.0 15.5 %copy-start = (bf16[640,1024]{0,1:T(8,128)(2,1)}, bf16[640,1024]{0,1:T(8,128)(2,1)S(1)}, u32[]{:S(2)}) copy-start(bf16[640,1024]{0,1:T(8,128)(2,1)S(1)} %get-tuple-element.2335) | copy-start | bytes 3932164
  264.5 12.0 copy-start.108
  264.5 12.0 copy-start.122
  267.1 9.4 copy-start.83
  285.9 22.9 %copy-start.109 = (f32[160,13]{0,1:T(8,128)S(1)}, f32[160,13]{0,1:T(8,128)}, u32[]{:S(2)}) copy-start(f32[160,13]{0,1:T(8,128)} %dynamic-slice_maximum_fusion.1) | copy-start | bytes 24964
  363.4 106.3 %reduce-scatter.9.cloned.1.call-start = ((), (), s32[]{:S(2)}) async-start(), calls=%async_computation.15 | async-start | bytes 3276800 | tf_op jit(solution)/shard_map/reduce_scatter | solution.py:295
  391.7 229.3 %all-gather.18.cloned.1.call-start = ((), (), s32[]{:S(2)}) async-start(), calls=%async_computation.10 | async-start | bytes 10485760 | tf_op jit(solution)/shard_map/all_gather | solution.py:208
  395.6 375.3 %all-gather.20.cloned.1.call-start = ((), (), s32[]{:S(2)}) async-start(), calls=%async_computation.11 | async-start | bytes 10485760 | tf_op jit(solution)/shard_map/all_gather | solution.py:208
  399.5 468.6 %reduce-scatter.13.cloned.1.call-start = ((), (), s32[]{:S(2)}) async-start(), calls=%async_computation.17 | async-start | bytes 2621440 | tf_op jit(solution)/shard_map/reduce_scatter | solution.py:338
  405.1 523.2 %reduce-scatter.11.cloned.1.call-start = ((), (), s32[]{:S(2)}) async-start(), calls=%async_computation.16 | async-start | bytes 7864320 | tf_op jit(solution)/shard_map/reduce_scatter | solution.py:338
  489.5 131.4 %copy-start.74 = (f32[1024]{0:T(1024)S(1)}, f32[1024]{0:T(1024)}, u32[]{:S(2)}) copy-start(f32[1024]{0:T(1024)} %get-tuple-element.1585) | copy-start | bytes 12292
  489.5 131.4 %copy-start.78 = (f32[1024]{0:T(1024)S(1)}, f32[1024]{0:T(1024)}, u32[]{:S(2)}) copy-start(f32[1024]{0:T(1024)} %get-tuple-element.1584) | copy-start | bytes 12292
  489.6 586.8 %reduce-scatter.15.cloned.1.call-start = ((), (), s32[]{:S(2)}) async-start(), calls=%async_computation.18 | async-start | bytes 10485760 | tf_op jit(solution)/shard_map/reduce_scatter | solution.py:338
  780.4 9.4 copy-start.30
  780.4 20.0 %slice-start = ((s8[8388608]{0:T(1024)(128)(4,1)}), s8[4194304]{0:T(1024)(128)(4,1)S(1)}, s32[]{:S(2)}) async-start(s8[8388608]{0:T(1024)(128)(4,1)} %bitcast.572), calls=%async_computation.21 | async-start | bytes 8388608
  789.8 10.6 slice-start.1
  819.5 404.9 %reduce-scatter.17.cloned.1.call-start = ((), (), s32[]{:S(2)}) async-start(), calls=%async_computation.19 | async-start | bytes 10485760 | tf_op jit(solution)/shard_map/reduce_scatter | solution.py:338
  819.6 9.1 copy-start.27
  840.3 492.9 %all-reduce.4.cloned.1.call-start = ((), (), s32[]{:S(2)}) async-start(), calls=%async_computation.20 | async-start | bytes 12582912 | tf_op jit(solution)/shard_map/psum | solution.py:341
  847.8 7.4 slice-start.2
  848.4 6.8 slice-start.3
  1224.4 32.0 %copy-start.87 = (f32[3328]{0:T(1024)S(1)}, f32[3328]{0:T(1024)}, u32[]{:S(2)}) copy-start(f32[3328]{0:T(1024)} %param.41) | copy-start | bytes 39940
  1224.4 32.0 %copy-start.98 = (f32[3328]{0:T(1024)S(1)}, f32[3328]{0:T(1024)}, u32[]{:S(2)}) copy-start(f32[3328]{0:T(1024)} %param.51) | copy-start | bytes 39940
  1224.4 32.0 %copy-start.99 = (f32[3328]{0:T(1024)S(1)}, f32[3328]{0:T(1024)}, u32[]{:S(2)}) copy-start(f32[3328]{0:T(1024)} %param.46) | copy-start | bytes 39940
  1257.2 76.0 %copy-start.29 = (f32[256,1024]{1,0:T(8,128)S(1)}, f32[256,1024]{1,0:T(8,128)}, u32[]{:S(2)}) copy-start(f32[256,1024]{1,0:T(8,128)} %param.38) | copy-start | bytes 3145732
  1356.8 6.8 copy-start.17
  1377.9 7.0 copy-start.18
  (106 other events, 279.5 us)
Sparse Core Ops, SparseCore 0:
  10.7 118.1 all-gather.9
  131.1 43.8 all-gather.15
  176.5 31.3 all-gather.23
  209.3 31.6 all-gather.21
  242.4 31.6 all-gather.13
  275.5 31.6 all-gather.11
  363.5 51.3 reduce-scatter.6
  417.8 51.8 reduce-scatter.8
  471.8 149.1 all-gather.17
  623.0 147.7 all-gather.19
  773.7 41.8 reduce-scatter.12
  818.3 109.9 reduce-scatter.10
  931.2 145.1 reduce-scatter.14
  1079.2 145.2 reduce-scatter.16
  1227.9 105.2 all-reduce.3
where the time goes:
time: 1410 us; the launch traced here: 1400 us
  waiting for transfers between devices  919 us (65%)
  matrix products  178 us (13%)
  local copies, waits for them, and re-layouts  125 us (9%)
  other arithmetic  107 us (8%)
  blocking collectives  46.7 us (3%)
  between operations  17 us (1%)
    all_gather x4, waiting for transfers between devices, local(): lax.all_gather(for_sending(owned_bf), 'shard', axis=0, tiled=True)  383 us
    reduce_scatter x4, waiting for transfers between devices, local(): lax.psum_scatter(for_sending(grad_totals), 'shard', scatter_dimension=0,...  356 us
    psum x1, waiting for transfers between devices, local(): lax.psum(for_sending(shard_sums), 'rep')  72.4 us
    another operation x13, other arithmetic, local(): states.append(jnp.stack([new_weight, new_average]))  55.1 us
    reduce_scatter x2, waiting for transfers between devices, local(): lax.psum_scatter(grad_kv_all.astype(jnp.bfloat16), 'shard', scatter_dimen...  45.7 us
    all_gather x2, waiting for transfers between devices, local(): lax.all_gather(value_rows, 'shard', axis=0, tiled=True)  45.5 us
    unnamed x273, local copies, waits for them, and re-layouts  28.8 us
  transfers between devices with their start and end apart: 15, of which 13 were waited for; matrix products, arithmetic and copies ran while one was open for 20% of the time, Pallas kernels for 0%

commit v1 on v0

v1 whole, which is shorter than its diff:
```python
from functools import partial
import math

import jax
import jax.numpy as jnp
from jax import lax
from jax.experimental import pallas as pl
from jax.experimental.pallas import tpu as pltpu
from jax.sharding import PartitionSpec as P

HEAD = 64
ROT = 16
PAIR = 2 * HEAD

EPSILON = 1e-05
NEGATIVE = -1e30
MOMENTUM = 0.5
AVERAGE_DECAY = 0.5
RATES = (0.045, 0.8, 0.1, 0.024, 0.4)

F32 = jnp.float32
BF16 = jnp.bfloat16
VMEM_LIMIT = 60 * 1024 * 1024


def dot(a, b):
    return jnp.dot(a, b, preferred_element_type=F32)


def dot_t(a, b):
    return lax.dot_general(a, b, (((1,), (1,)), ((), ())), preferred_element_type=F32)


def normalize(values):
    center = values - jnp.mean(values, axis=-1, keepdims=True)
    spread = lax.rsqrt(jnp.mean(center * center, axis=-1, keepdims=True) + EPSILON)
    return center * spread, spread


def fixed(shape, index=None):
    zeros = (0,) * len(shape) if index is None else index
    return pl.BlockSpec(shape, lambda i: zeros, pipeline_mode=pl.Buffered(1))


def rows_of(ref):
    block = ref[...]
    return block.reshape(-1, block.shape[-1])


def mlp_kernel(first, reps, shards, *refs):
    if first:
        (x_ref, dy_ref, gain_ref, bias_ref, ub_ref, up_ref, down_ref,
         out_ref, dx_ref, dup_ref, ddown_ref, dub_ref, sums_ref,
         hid, hid_t, unit, acc_out, acc_dx) = refs
    else:
        (x_ref, dy_ref, gain_ref, bias_ref, ub_ref, up_ref, down_ref, pup_ref, pdown_ref, pub_ref,
         out_ref, dx_ref, dup_ref, ddown_ref, dub_ref, sums_ref,
         hid, hid_t, unit, acc_out, acc_dx) = refs
    step = pl.program_id(0)

    @pl.when(step == 0)
    def _():
        xhat, _ = normalize(rows_of(x_ref).astype(F32))
        unit[...] = xhat
        h = (xhat * gain_ref[...] + bias_ref[...]).astype(BF16)
        hid[...] = h
        hid_t[...] = h.T
        acc_out[...] = jnp.zeros_like(acc_out)
        acc_dx[...] = jnp.zeros_like(acc_dx)

    dy = rows_of(dy_ref)
    up = up_ref[...]
    down = down_ref[...]
    u = dot(hid[...], up) + ub_ref[...]
    cdf = 0.5 * (1.0 + lax.erf(u * (0.5 ** 0.5)))
    act = (u * cdf).astype(BF16)
    slope = cdf + u * (jnp.exp(-0.5 * u * u) * ((2.0 * math.pi) ** -0.5))
    dact = dot_t(dy, down)
    du32 = dact * slope
    du = du32.astype(BF16)
    acc_out[...] += dot(act, down)
    acc_dx[...] += dot_t(du, up)
    ddown = dot(act.T, dy)
    dup = dot(hid_t[...], du)
    dub = jnp.sum(du.astype(F32), axis=0, keepdims=True)
    if not first:
        ddown = ddown + pdown_ref[...]
        dub = dub + pub_ref[...]
    ddown_ref[...] = ddown.astype(ddown_ref.dtype)
    dub_ref[...] = dub
    if first:
        dup_ref[...] = dup
    else:
        dup = dup + pup_ref[...]
        part = dup.shape[0] // shards
        for z in range(shards):
            dup_ref[:, z] = dup[z * part:(z + 1) * part].reshape(
                reps, part // reps, dup.shape[1]).astype(BF16)

    @pl.when(step == pl.num_programs(0) - 1)
    def _():
        dh = acc_dx[...]
        out_ref[...] = acc_out[...]
        dx_ref[...] = dh * gain_ref[...]
        sums_ref[0:1] = jnp.sum(dh * unit[...], axis=0, keepdims=True)
        sums_ref[1:2] = jnp.sum(dh, axis=0, keepdims=True)
        sums_ref[2:3] = jnp.sum(dy.astype(F32), axis=0, keepdims=True)
        sums_ref[3:8] = jnp.zeros((5, dh.shape[1]), F32)


def mlp_call(xy, gain, bias, up_bias, weights, down, previous, reps, shards, first_col):
    _, _, rows, width = xy.shape
    tokens = shards * rows
    hidden = down.shape[0]
    block = 256 if hidden % 256 == 0 and first_col % 256 == 0 else 128
    steps = hidden // block
    offset = first_col // block
    first = previous is None
    whole = lambda i: (0, 0)
    in_specs = [
        fixed((shards, 1, rows, width)),
        fixed((shards, 1, rows, width), (0, 1, 0, 0)),
        fixed((1, width)),
        fixed((1, width)),
        pl.BlockSpec((1, block), lambda i: (0, i)),
        pl.BlockSpec((width, block), lambda i: (0, offset + i)),
        pl.BlockSpec((block, width), lambda i: (i, 0)),
    ]
    args = [xy, xy, gain, bias, up_bias, weights, down]
    if first:
        dup_shape = jax.ShapeDtypeStruct((width, hidden), F32)
        dup_spec = pl.BlockSpec((width, block), lambda i: (0, i))
    else:
        in_specs += [
            pl.BlockSpec((width, block), lambda i: (0, i)),
            pl.BlockSpec((block, width), lambda i: (i, 0)),
            pl.BlockSpec((1, block), lambda i: (0, i)),
        ]
        args += list(previous)
        part = width // shards // reps
        dup_shape = jax.ShapeDtypeStruct((reps, shards, part, hidden), BF16)
        dup_spec = pl.BlockSpec((reps, shards, part, block), lambda i: (0, 0, 0, i))
    return pl.pallas_call(
        partial(mlp_kernel, first, reps, shards),
        grid=(steps,),
        in_specs=in_specs,
        out_specs=[
            pl.BlockSpec((tokens, width), whole),
            pl.BlockSpec((tokens, width), whole),
            dup_spec,
            pl.BlockSpec((block, width), lambda i: (i, 0)),
            pl.BlockSpec((1, block), lambda i: (0, i)),
            pl.BlockSpec((8, width), whole),
        ],
        out_shape=[
            jax.ShapeDtypeStruct((tokens, width), F32),
            jax.ShapeDtypeStruct((tokens, width), F32),
            dup_shape,
            jax.ShapeDtypeStruct((hidden, width), F32 if first else BF16),
            jax.ShapeDtypeStruct((1, hidden), F32),
            jax.ShapeDtypeStruct((8, width), F32),
        ],
        scratch_shapes=[
            pltpu.VMEM((tokens, width), BF16),
            pltpu.VMEM((width, tokens), BF16),
            pltpu.VMEM((tokens, width), F32),
            pltpu.VMEM((tokens, width), F32),
            pltpu.VMEM((tokens, width), F32),
        ],
        compiler_params=pltpu.CompilerParams(
            dimension_semantics=("arbitrary",), vmem_limit_bytes=VMEM_LIMIT),
        cost_estimate=pl.CostEstimate(
            flops=12 * tokens * width * hidden, bytes_accessed=24 * 2**20,
            transcendentals=2 * tokens * hidden),
    )(*args)


def swap_halves(values):
    half = ROT // 2
    lane = lax.broadcasted_iota(jnp.int32, values.shape, 1) % HEAD
    return jnp.where(lane < half, pltpu.roll(values, PAIR - half, 1), pltpu.roll(values, half, 1))


def attn_kernel(first, reps, shards, *refs):
    if first:
        (x_ref, dy_ref, gain_ref, bias_ref, cos_ref, sin_ref, mask_ref, qb_ref, qkv_ref, wo_ref,
         out_ref, dx_ref,
         send_ref, dqkv_ref, dwo_ref, dqb_ref, sums_ref,
         hid, hid_t, unit, acc_out, acc_dh) = refs
    else:
        (x_ref, dy_ref, gain_ref, bias_ref, cos_ref, sin_ref, mask_ref, qb_ref, qkv_ref, wo_ref,
         out_ref, dx_ref, pqkv_ref, pwo_ref, pqb_ref,
         send_ref, dqkv_ref, dwo_ref, dqb_ref, sums_ref,
         hid, hid_t, unit, acc_out, acc_dh) = refs
    step = pl.program_id(0)

    @pl.when(step == 0)
    def _():
        xhat, _ = normalize(rows_of(x_ref).astype(F32))
        unit[...] = xhat
        h = (xhat * gain_ref[...] + bias_ref[...]).astype(BF16)
        hid[...] = h
        hid_t[...] = h.T
        acc_out[...] = out_ref[...]
        acc_dh[...] = jnp.zeros_like(acc_dh)

    dy = rows_of(dy_ref)
    weights = qkv_ref[...]
    wo = wo_ref[...]
    cosine = cos_ref[...]
    sine = sin_ref[...]
    lin = dot(hid[...], weights) + qb_ref[...]
    q32 = lin[:, :PAIR]
    k32 = lin[:, PAIR:2 * PAIR]
    q = (q32 * cosine + swap_halves(q32) * sine).astype(BF16) * BF16(HEAD ** -0.5)
    k = (k32 * cosine + swap_halves(k32) * sine).astype(BF16)
    v = lin[:, 2 * PAIR:].astype(BF16)
    do = dot_t(dy, wo).astype(BF16)
    k_t = k.T
    v_t = v.T
    lane = lax.broadcasted_iota(jnp.int32, q.shape, 1)
    o_parts = []
    dq_parts = []
    dk = None
    dv = None
    tokens = q.shape[0]
    chunk = tokens if tokens <= 640 else tokens // 2
    for head in range(2):
        own = (lane // HEAD) == head
        q_h = jnp.where(own, q, jnp.zeros_like(q))
        do_h = jnp.where(own, do, jnp.zeros_like(do))
        part = slice(head * HEAD, (head + 1) * HEAD)
        o_row = []
        dq_row = []
        for at in range(0, tokens, chunk):
            q_c = q_h[at:at + chunk]
            do_c = do_h[at:at + chunk]
            scores = dot_t(k, q_c) + mask_ref[:, at:at + chunk]
            top = jnp.max(scores, axis=0, keepdims=True)
            e = jnp.exp(scores - top)
            prob = e * (1.0 / jnp.sum(e, axis=0, keepdims=True))
            prob_bf = prob.astype(BF16)
            o_row.append(dot(v_t[part], prob_bf))
            dprob = dot_t(v, do_c)
            weighted = prob * dprob
            delta = jnp.sum(weighted, axis=0, keepdims=True)
            ds = (weighted - prob * delta).astype(BF16)
            dq_row.append(dot(k_t[part], ds))
            dk_c = dot(ds, q_c)
            dv_c = dot(prob_bf, do_c)
            dk = dk_c if dk is None else dk + dk_c
            dv = dv_c if dv is None else dv + dv_c
        o_parts.append(jnp.concatenate(o_row, axis=1))
        dq_parts.append(jnp.concatenate(dq_row, axis=1))
    o_t = jnp.concatenate(o_parts, axis=0).astype(BF16)
    dq = jnp.concatenate(dq_parts, axis=0).T * (HEAD ** -0.5)
    dq = dq * cosine - swap_halves(dq) * sine
    dk = dk * cosine - swap_halves(dk) * sine
    dqkv = jnp.concatenate([dq.astype(BF16), dk.astype(BF16), dv.astype(BF16)], axis=1)
    acc_out[...] += dot(o_t.T, wo)
    acc_dh[...] += dot_t(dqkv, weights)
    dwo = dot(o_t, dy)
    dw = dot(hid_t[...], dqkv)
    dqb = jnp.sum(dqkv.astype(F32), axis=0, keepdims=True)
    if first:
        dwo_ref[...] = dwo
        dqkv_ref[...] = dw
        dqb_ref[...] = dqb
    else:
        dwo_ref[...] = (dwo + pwo_ref[...]).astype(BF16)
        dqb_ref[...] = dqb + pqb_ref[...]
        dw = dw + pqkv_ref[...]
        part = dw.shape[0] // shards
        for z in range(shards):
            dqkv_ref[:, z] = dw[z * part:(z + 1) * part].reshape(
                reps, part // reps, dw.shape[1]).astype(BF16)

    @pl.when(step == pl.num_programs(0) - 1)
    def _():
        rows = send_ref.shape[2]
        width = send_ref.shape[3]
        dh = acc_dh[...]
        send_ref[:, 0] = acc_out[...].astype(BF16).reshape(shards, rows, width)
        send_ref[:, 1] = (dx_ref[...] + dh * gain_ref[...]).astype(BF16).reshape(
            shards, rows, width)
        sums_ref[0:1] = jnp.sum(dh * unit[...], axis=0, keepdims=True)
        sums_ref[1:2] = jnp.sum(dh, axis=0, keepdims=True)
        sums_ref[2:8] = jnp.zeros((6, width), F32)


def attn_call(xy, gain, bias, cosine, sine, mask, qkv_bias, weights, wo, partials, previous,
              reps, shards):
    _, _, rows, width = xy.shape
    tokens = shards * rows
    pairs = wo.shape[0] // PAIR
    cols = 3 * PAIR
    first = previous is None
    whole = lambda i: (0, 0)
    in_specs = [
        fixed((shards, 1, rows, width)),
        fixed((shards, 1, rows, width), (0, 1, 0, 0)),
        fixed((1, width)),
        fixed((1, width)),
        fixed((tokens, PAIR)),
        fixed((tokens, PAIR)),
        fixed((tokens, tokens)),
        pl.BlockSpec((1, cols), lambda i: (0, i)),
        pl.BlockSpec((width, cols), lambda i: (0, i)),
        pl.BlockSpec((PAIR, width), lambda i: (i, 0)),
        fixed((tokens, width)),
        fixed((tokens, width)),
    ]
    args = [xy, xy, gain, bias, cosine, sine, mask, qkv_bias, weights, wo, *partials]
    if first:
        dqkv_shape = jax.ShapeDtypeStruct((width, pairs * cols), F32)
        dqkv_spec = pl.BlockSpec((width, cols), lambda i: (0, i))
    else:
        in_specs += [
            pl.BlockSpec((width, cols), lambda i: (0, i)),
            pl.BlockSpec((PAIR, width), lambda i: (i, 0)),
            pl.BlockSpec((1, cols), lambda i: (0, i)),
        ]
        args += list(previous)
        part = width // shards // reps
        dqkv_shape = jax.ShapeDtypeStruct((reps, shards, part, pairs * cols), BF16)
        dqkv_spec = pl.BlockSpec((reps, shards, part, cols), lambda i: (0, 0, 0, i))
    return pl.pallas_call(
        partial(attn_kernel, first, reps, shards),
        grid=(pairs,),
        in_specs=in_specs,
        out_specs=[
            pl.BlockSpec((shards, 2, rows, width), lambda i: (0, 0, 0, 0)),
            dqkv_spec,
            pl.BlockSpec((PAIR, width), lambda i: (i, 0)),
            pl.BlockSpec((1, cols), lambda i: (0, i)),
            pl.BlockSpec((8, width), whole),
        ],
        out_shape=[
            jax.ShapeDtypeStruct((shards, 2, rows, width), BF16),
            dqkv_shape,
            jax.ShapeDtypeStruct((pairs * PAIR, width), F32 if first else BF16),
            jax.ShapeDtypeStruct((1, pairs * cols), F32),
            jax.ShapeDtypeStruct((8, width), F32),
        ],
        scratch_shapes=[
            pltpu.VMEM((tokens, width), BF16),
            pltpu.VMEM((width, tokens), BF16),
            pltpu.VMEM((tokens, width), F32),
            pltpu.VMEM((tokens, width), F32),
            pltpu.VMEM((tokens, width), F32),
        ],
        compiler_params=pltpu.CompilerParams(
            dimension_semantics=("arbitrary",), vmem_limit_bytes=VMEM_LIMIT),
        cost_estimate=pl.CostEstimate(
            flops=pairs * (6 * tokens * width * 4 * PAIR + 28 * tokens * tokens * PAIR),
            bytes_accessed=20 * 2**20, transcendentals=2 * pairs * tokens * tokens),
    )(*args)


def rotation_tables(pos_ids):
    half = ROT // 2
    lane = jnp.arange(PAIR, dtype=jnp.int32) % HEAD
    frequency = 10000.0 ** (-(jnp.arange(half, dtype=F32) * 2.0) / ROT)
    per_lane = jnp.where(lane < ROT, frequency[lane % half], 0.0)
    sign = jnp.where(lane < half, -1.0, jnp.where(lane < ROT, 1.0, 0.0))
    angles = pos_ids.astype(F32)[:, None] * per_lane[None, :]
    return jnp.cos(angles), jnp.sin(angles) * sign[None, :]


def visible_bias(seg_ids, pos_ids, par_ids):
    labels = jnp.arange(par_ids.shape[0], dtype=jnp.int32)
    own = seg_ids[:, None] == labels[None, :]
    parent = jnp.sum(jnp.where(own, par_ids[None, :], 0), axis=1)
    parent_hot = parent[:, None] == labels[None, :]
    grand = jnp.sum(jnp.where(parent_hot, par_ids[None, :], 0), axis=1)
    key_seg = seg_ids[:, None]
    reach = (
        (key_seg == seg_ids[None, :])
        | (key_seg == parent[None, :])
        | (key_seg == grand[None, :])
    )
    return jnp.where(reach & (pos_ids[:, None] <= pos_ids[None, :]), 0.0, NEGATIVE).astype(F32)


def local(
    block_input,
    out_cotangent,
    segment_ids,
    positions,
    parent_ids,
    qkv_weight,
    attn_weight,
    up_weight,
    down_weight,
    small_params,
    qkv_moment,
    attn_moment,
    up_moment,
    down_moment,
    small_moment,
    qkv_average,
    attn_average,
    up_average,
    down_average,
    small_average,
):
    shards = lax.axis_size("shard")
    reps = lax.axis_size("rep")
    me = lax.axis_index("rep")
    z = lax.axis_index("shard")
    micro_count, rows, width = block_input.shape
    hidden = up_weight.shape[1]
    part = qkv_weight.shape[0] // reps
    slice_ff = hidden // shards
    slice_d = width // shards
    pairs = slice_d // PAIR
    qkv_cols = 3 * slice_d

    qkv_rows = lax.dynamic_slice_in_dim(qkv_weight, me * part, part, 0).astype(BF16)
    up_rows = lax.dynamic_slice_in_dim(up_weight, me * part, part, 0).astype(BF16)
    qkv_rows = qkv_rows.reshape(part, 3, shards, pairs, PAIR).transpose(2, 0, 3, 1, 4)
    up_rows = up_rows.reshape(part, shards, slice_ff).transpose(1, 0, 2)
    outgoing = jnp.concatenate([qkv_rows.reshape(shards, part, qkv_cols), up_rows], axis=2)
    arrived = lax.all_to_all(outgoing, "shard", 0, 0, tiled=False)
    weights = lax.all_gather(arrived, "rep", axis=1).reshape(width, qkv_cols + slice_ff)
    down_bf = down_weight.astype(BF16)
    attn_bf = attn_weight.astype(BF16)

    small_full = lax.all_gather(small_params.astype(BF16), "shard", axis=0, tiled=True).astype(F32)
    gain_one, bias_one, gain_two, bias_two = (
        small_full[i * width:(i + 1) * width].reshape(1, width) for i in range(4))
    qkv_bias = small_full[4 * width:7 * width].reshape(3, shards, pairs, PAIR)
    qkv_bias = lax.dynamic_index_in_dim(qkv_bias, z, 1, keepdims=False)
    qkv_bias = qkv_bias.transpose(1, 0, 2).reshape(1, qkv_cols)
    attn_bias = small_full[7 * width:8 * width]
    up_bias = lax.dynamic_slice_in_dim(
        small_full[8 * width:8 * width + hidden], z * slice_ff, slice_ff, 0).reshape(1, slice_ff)
    down_bias = small_full[8 * width + hidden:]

    mlp_previous = None
    attn_previous = None
    sums_two = 0.0
    sums_one = 0.0
    summed = []
    for m in range(micro_count):
        pair = jnp.stack([block_input[m], out_cotangent[m]])
        xy = lax.all_gather(pair, "shard", axis=0)
        cosine, sine = rotation_tables(positions[m])
        mask = visible_bias(segment_ids[m], positions[m], parent_ids[m, 0])
        out_part, dx_part, *mlp_previous, sums = mlp_call(
            xy, gain_two, bias_two, up_bias, weights, down_bf, mlp_previous, reps, shards, qkv_cols)
        sums_two = sums_two + sums
        send, *attn_previous, sums = attn_call(
            xy, gain_one, bias_one, cosine, sine, mask, qkv_bias, weights, attn_bf,
            (out_part, dx_part), attn_previous, reps, shards)
        sums_one = sums_one + sums
        summed.append(lax.psum_scatter(send, "shard", scatter_dimension=0, tiled=False))

    grad_up, grad_down, grad_up_bias = mlp_previous
    grad_qkv, grad_attn, grad_qkv_bias = attn_previous

    grad_down = lax.psum_scatter(
        grad_down.reshape(reps, -1, width), "rep", scatter_dimension=0, tiled=False)
    grad_attn = lax.psum_scatter(
        grad_attn.reshape(reps, -1, width), "rep", scatter_dimension=0, tiled=False)
    grad_up = lax.psum_scatter(grad_up, "rep", scatter_dimension=0, tiled=False)
    grad_qkv = lax.psum_scatter(grad_qkv, "rep", scatter_dimension=0, tiled=False)
    grad_up = lax.all_to_all(grad_up, "shard", 0, 0, tiled=False)
    grad_qkv = lax.all_to_all(grad_qkv, "shard", 0, 0, tiled=False)
    full_down = lax.all_gather(grad_down, "rep", axis=0, tiled=True)
    full_attn = lax.all_gather(grad_attn, "rep", axis=0, tiled=True)
    full_up = lax.all_gather(grad_up, "rep", axis=0).transpose(0, 2, 1, 3).reshape(-1, hidden)
    full_qkv = lax.all_gather(grad_qkv, "rep", axis=0)
    full_qkv = full_qkv.reshape(reps, shards, part, pairs, 3, PAIR).transpose(0, 2, 4, 1, 3, 5)
    full_qkv = full_qkv.reshape(-1, 3 * width)

    head_part = jnp.concatenate(
        [sums_one[0], sums_one[1], sums_two[0], sums_two[1]])
    bias_part = lax.dynamic_update_slice(
        jnp.zeros((3, shards, slice_d), F32),
        grad_qkv_bias.reshape(pairs, 3, PAIR).transpose(1, 0, 2).reshape(3, 1, slice_d),
        (0, z, 0)).reshape(-1)
    token_part = jnp.where(z == 0, sums_two[2], 0.0)
    ff_part = lax.dynamic_update_slice(
        jnp.zeros((hidden,), F32), grad_up_bias.reshape(-1), (z * slice_ff,))
    small_grad = lax.psum(
        jnp.concatenate([head_part, bias_part, token_part, ff_part, token_part]), ("rep", "shard"))
    count = small_params.shape[0]
    small_grad = lax.dynamic_slice_in_dim(small_grad, z * count, count, 0)

    block_outputs = []
    input_grads = []
    for m in range(micro_count):
        x32 = block_input[m].astype(F32)
        block_outputs.append(
            (x32 + summed[m][0].astype(F32) + (attn_bias + down_bias)[None, :]).astype(BF16))
        unit, spread = normalize(x32)
        scaled = summed[m][1].astype(F32)
        input_grads.append(
            out_cotangent[m].astype(F32) + spread * (
                scaled - jnp.mean(scaled, axis=-1, keepdims=True)
                - unit * jnp.mean(scaled * unit, axis=-1, keepdims=True)))

    grads = [full_qkv.astype(F32), full_attn.astype(F32), full_up.astype(F32),
             full_down.astype(F32), small_grad]
    all_tok = micro_count * rows * shards * reps
    masters = (qkv_weight, attn_weight, up_weight, down_weight, small_params)
    moments = (qkv_moment, attn_moment, up_moment, down_moment, small_moment)
    averages = (qkv_average, attn_average, up_average, down_average, small_average)
    states = []
    new_moments = []
    for weight_index in range(5):
        gradient = grads[weight_index]
        new_moment = MOMENTUM * moments[weight_index] + gradient
        rate_now = RATES[weight_index] / math.sqrt(all_tok)
        new_weight = masters[weight_index] - rate_now * (gradient + MOMENTUM * new_moment)
        new_average = AVERAGE_DECAY * averages[weight_index] + (1.0 - AVERAGE_DECAY) * new_weight
        states.append(jnp.stack([new_weight, new_average]))
        new_moments.append(new_moment)
    return (
        jnp.stack(block_outputs),
        jnp.stack(input_grads),
        *grads,
        *states,
        *new_moments,
    )


def solution(mesh):
    tokens = P(None, ("rep", "shard"), None)
    tree = P(None, "rep")
    matrix = P("shard", None)
    vector = P("shard")
    weights = (matrix, matrix, matrix, matrix, vector)
    state = P(None, "shard", None)
    return jax.shard_map(
        local,
        mesh=mesh,
        in_specs=(tokens, tokens, tree, tree, P(None, "rep", None), *weights, *weights, *weights),
        out_specs=(tokens, tokens, *weights, state, state, state, state, P(None, "shard"),
                   *weights),
        check_vma=False,
    )
```

time: 1410 us -> 640 us (0.45)
  waiting for transfers between devices: 919 us -> 297 us
  matrix products: 178 us -> 0 us
  local copies, waits for them, and re-layouts: 125 us -> 30.4 us
  Pallas kernels: 0 us -> 79.1 us
  blocking collectives: 46.7 us -> 108 us
    all_gather x8 -> x6, waiting for transfers between devices: 444 us -> 101 us  [the longest x2 39.9 us: local(): xy = lax.all_gather(pair, 'shard', axis=0)]
    reduce_scatter x6, waiting for transfers between devices: 402 us -> 183 us  [the longest x2 89.7 us: local(): lax.psum_scatter(send, 'shard', scatter_dimension=0, tiled=False)]
    dot_general x68 -> x0, matrix products: 178 us -> none  [the longest x2 21.7 us: local(): jnp.dot(second_bf, up_full, preferred_element_type=jnp.float32) + up_bias]
    pallas_call x0 -> x4, Pallas kernels: none -> 79.1 us  [the longest x2 44.6 us: attn_call(): pl.pallas_call(partial(attn_kernel, first, reps, shards), grid=(pairs,),...]
    psum x1 -> x0, waiting for transfers between devices: 72.4 us -> none  [local(): lax.psum(for_sending(shard_sums), 'rep')]
    all_to_all x0 -> x2, blocking collectives: none -> 43 us  [the longest x1 30.8 us: local(): arrived = lax.all_to_all(outgoing, 'shard', 0, 0, tiled=False)]
    dynamic_slice x32 -> x1, local copies, waits for them, and re-layouts: 28.6 us -> 0.59 us  [local(): lax.dynamic_slice_in_dim(small_full[8 * width:8 * width + hidden], z * sl...]
    psum x1, blocking collectives: 13.4 us -> 39.9 us  [local(): lax.psum(jnp.concatenate([head_part, bias_part, token_part, ff_part, toke...]
  transfers between devices with their start and end apart: 15 -> 13, of which waited for: 13 -> 11; matrix products, arithmetic and copies ran while one was open for 20% -> 14% of each run, Pallas kernels for 0% -> 3%
where the time goes in v1:
time: 640 us; the launch traced here: 630 us
  waiting for transfers between devices  297 us (46%)
  blocking collectives  108 us (17%)
  other arithmetic  94.4 us (15%)
  Pallas kernels  79.1 us (12%)
  local copies, waits for them, and re-layouts  30.4 us (5%)
  between operations  15.3 us (2%)
    reduce_scatter x2, waiting for transfers between devices, local(): lax.psum_scatter(send, 'shard', scatter_dimension=0, tiled=False)  89.7 us
    another operation x13, other arithmetic, local(): states.append(jnp.stack([new_weight, new_average]))  62.7 us
    pallas_call x2, Pallas kernels, attn_call(): pl.pallas_call(partial(attn_kernel, first, reps, shards), grid=(pairs,),...  44.6 us
    all_gather x2, waiting for transfers between devices, local(): xy = lax.all_gather(pair, 'shard', axis=0)  39.9 us
    psum x1, blocking collectives, local(): lax.psum(jnp.concatenate([head_part, bias_part, token_part, ff_part, toke...  39.9 us
    pallas_call x2, Pallas kernels, mlp_call(): pl.pallas_call(partial(mlp_kernel, first, reps, shards), grid=(steps,), i...  34.5 us
    reduce_scatter x1, waiting for transfers between devices, local(): lax.psum_scatter(grad_qkv, 'rep', scatter_dimension=0, tiled=False)  33.8 us
    reduce_scatter x1, waiting for transfers between devices, local(): lax.psum_scatter(grad_down.reshape(reps, -1, width), 'rep', scatter_dimen...  32.6 us
  transfers between devices with their start and end apart: 13, of which 11 were waited for; matrix products, arithmetic and copies ran while one was open for 14% of the time, Pallas kernels for 3%

profile of v1, /device:TPU:0, one launch (start us, length us, event | category | flops | bytes accessed | tf_op | source)
XLA Modules:
  0.0 629.5 jit_solution(7027363142916374140)
XLA Ops:
  7.2 1.4 fusion.36
  12.3 30.8 %all_to_all.15 = bf16[4,32,1792]{2,1,0:T(8,128)(2,1)} all-to-all(bf16[4,32,1792]{2,1,0:T(8,128)(2,1)S(1)} %pad_maximum_fusion.8), channel_id=1, replica_groups=mesh['rep'=8,'shard'=4] {'shard'}, dimensions={0} | all-to-all | bytes 917504 | tf_op jit(solution)/shard_map/all_to_all | solution.py:424
  44.2 14.2 %all-gather.7 = bf16[4,1,3328]{2,1,0:T(2,128)(2,1)S(1)} all-gather(bf16[1,1,3328]{2,1,0:T(2,128)(2,1)S(1)} %reshape.491), channel_id=1, replica_groups=mesh['rep'=8,'shard'=4] {'shard'}, dimensions={0}, use_global_device_ids=true | all-gather | bytes 33280 | tf_op jit(solution)/shard_map/all_gather | solution.py:429
  60.1 3.8 convert_element_type.160.refs_6_
  65.1 5.2 compare_select_fusion.9
  71.3 3.6 fusion.28
  74.9 1.6 and_select_fusion.1.refs_6_
  76.5 1.7 and_select_fusion.refs_6_
  78.2 32.2 %all-gather.17.cloned.1.call-done = bf16[4,256,1792]{2,1,0:T(8,128)(2,1)} async-done(((bf16[4,32,1792]{2,1,0:T(8,128)(2,1)}), bf16[4,256,1792]{2,1,0:T(8,128)(2,1)}) %all-gather.17.cloned.1.call-update) | async-done | bytes 3670032 | tf_op jit(solution)/shard_map/all_gather | solution.py:425
  110.4 17.0 %shard_map.323 = (f32[640,1024]{1,0:T(8,128)}, f32[640,1024]{1,0:T(8,128)}, f32[1024,1024]{1,0:T(8,128)}, f32[1024,1024]{1,0:T(8,128)}, f32[1,1024]{1,0:T(1,128)}, /*index=5*/f32[8,1024]{1,0:T(8,128)}) custom-call(bf16[4,2,160,1024]{3,2,1,0:T(8,128)(2,1)} %bitcast.200, bf16[4,2,160,1024]{3,2,1,0:T(8,128)(2,1)} %bitcast.201, f32[1,1024]{1,0:T(1,128)} %bitcast.194, ...), custom_call_target="tpu_custom_call" | custom-call | flops 8053063680 | bytes 25165824 | tf_op jit(solution)/shard_map/pallas_call | solution.py:143
  127.5 39.9 %all-gather.19.cloned.1.call-done = bf16[8,160,1024]{2,1,0:T(8,128)(2,1)} async-done(((bf16[2,160,1024]{2,1,0:T(8,128)(2,1)}), bf16[8,160,1024]{2,1,0:T(8,128)(2,1)}) %all-gather.19.cloned.1.call-update) | async-done | bytes 2621456 | tf_op jit(solution)/shard_map/all_gather | solution.py:447
  167.4 17.5 %shard_map.325 = (f32[640,1024]{1,0:T(8,128)}, f32[640,1024]{1,0:T(8,128)}, bf16[8,4,32,1024]{3,2,1,0:T(8,128)(2,1)}, bf16[1024,1024]{1,0:T(8,128)(2,1)}, f32[1,1024]{1,0:T(1,128)}, /*index=5*/f32[8,1024]{1,0:T(8,128)}) custom-call(bf16[4,2,160,1024]{3,2,1,0:T(8,128)(2,1)} %bitcast.204, bf16[4,2,160,1024]{3,2,1,0:T(8,128)(2,1)} %bitcast.205, ...), custom_call_target="tpu_custom_call" | custom-call | flops 8053063680 | bytes 25165824 | tf_op jit(solution)/shard_map/pallas_call | solution.py:143
  184.8 22.0 %shard_map.324 = (bf16[4,2,160,1024]{3,2,1,0:T(8,128)(2,1)}, f32[1024,768]{1,0:T(8,128)}, f32[256,1024]{1,0:T(8,128)}, f32[1,768]{1,0:T(1,128)}, f32[8,1024]{1,0:T(8,128)}) custom-call(bf16[4,2,160,1024]{3,2,1,0:T(8,128)(2,1)} %bitcast.202, bf16[4,2,160,1024]{3,2,1,0:T(8,128)(2,1)} %bitcast.203, f32[1,1024]{1,0:T(1,128)} %bitcast.190, f32[1,1024]{1,0:T(1,128)} %bitcast.188, ...), custom_call_target="tpu_custom_call" | custom-call | flops 6962544640 | bytes 20971520 | tf_op jit(solution)/shard_map/pallas_call | solution.py:327
  206.9 22.6 %shard_map.326 = (bf16[4,2,160,1024]{3,2,1,0:T(8,128)(2,1)}, bf16[8,4,32,768]{3,2,1,0:T(8,128)(2,1)}, bf16[256,1024]{1,0:T(8,128)(2,1)}, f32[1,768]{1,0:T(1,128)}, f32[8,1024]{1,0:T(8,128)}) custom-call(bf16[4,2,160,1024]{3,2,1,0:T(8,128)(2,1)} %bitcast.206, bf16[4,2,160,1024]{3,2,1,0:T(8,128)(2,1)} %bitcast.207, f32[1,1024]{1,0:T(1,128)} %bitcast.191, ...), custom_call_target="tpu_custom_call" | custom-call | flops 6962544640 | bytes 20971520 | tf_op jit(solution)/shard_map/pallas_call | solution.py:327
  233.0 33.8 %reduce-scatter.11.cloned.1.call-done = bf16[1,4,32,768]{3,2,1,0:T(8,128)(2,1)} async-done(((bf16[8,4,32,768]{3,2,1,0:T(8,128)(2,1)}), bf16[1,4,32,768]{3,2,1,0:T(8,128)(2,1)}) %reduce-scatter.11.cloned.1.call-update) | async-done | bytes 196624 | tf_op jit(solution)/shard_map/reduce_scatter | solution.py:467
  266.7 12.2 %all_to_all.16 = bf16[4,32,768]{2,1,0:T(8,128)(2,1)} all-to-all(bf16[4,32,768]{2,1,0:T(8,128)(2,1)} %bitcast.174), channel_id=1, replica_groups=mesh['rep'=8,'shard'=4] {'shard'}, dimensions={0} | all-to-all | bytes 393216 | tf_op jit(solution)/shard_map/all_to_all | solution.py:469
  279.0 32.6 %reduce-scatter.17.cloned.1.call-done = bf16[1,128,1024]{2,1,0:T(8,128)(2,1)} async-done(((bf16[8,128,1024]{2,1,0:T(8,128)(2,1)}), bf16[1,128,1024]{2,1,0:T(8,128)(2,1)}) %reduce-scatter.17.cloned.1.call-update) | async-done | bytes 262160 | tf_op jit(solution)/shard_map/reduce_scatter | solution.py:462
  312.7 39.9 %psum.7 = f32[13312]{0:T(1024)S(1)} all-reduce(f32[13312]{0:T(1024)S(1)} %constant_dynamic-update-slice_fusion), channel_id=1, replica_groups=mesh['rep'=8,'shard'=4] {'rep','shard'}, use_global_device_ids=true, to_apply=%region_18.19 | all-reduce | flops 13312 | bytes 106496 | tf_op jit(solution)/shard_map/psum | solution.py:486
  354.0 10.9 %all-gather.4 = bf16[1,256,1024]{2,1,0:T(8,128)(2,1)S(1)} all-gather(bf16[1,32,1024]{2,1,0:T(8,128)(2,1)} %reduce-scatter.13.cloned.1.call-done), channel_id=6, replica_groups=mesh['rep'=8,'shard'=4] {'rep'}, dimensions={1}, use_global_device_ids=true | all-gather | bytes 589824 | tf_op jit(solution)/shard_map/all_gather | solution.py:471
  364.9 3.0 fusion.32
  367.9 26.5 %reduce-scatter.15.cloned.1.call-done = bf16[1,4,32,1024]{3,2,1,0:T(8,128)(2,1)} async-done(((bf16[8,4,32,1024]{3,2,1,0:T(8,128)(2,1)}), bf16[1,4,32,1024]{3,2,1,0:T(8,128)(2,1)}) %reduce-scatter.15.cloned.1.call-update) | async-done | bytes 262160 | tf_op jit(solution)/shard_map/reduce_scatter | solution.py:466
  394.4 4.6 all-to-all-start.2
  399.1 2.1 multiply_bitcast_fusion.3
  401.2 1.5 pad_maximum_fusion.3
  402.7 10.1 %all-to-all-done.2 = bf16[4,32,1024]{2,1,0:T(8,128)(2,1)S(1)} async-done(((bf16[4,32,1024]{2,1,0:T(8,128)(2,1)}), bf16[4,32,1024]{2,1,0:T(8,128)(2,1)S(1)}, u32[]{:S(2)}, u32[]{:S(2)}) %all-to-all-start.2) | async-done | bytes 262176 | tf_op jit(solution)/shard_map/all_to_all | solution.py:468
  413.5 36.2 %reduce-scatter.7.cloned.1.call-done = bf16[1,2,160,1024]{3,2,1,0:T(8,128)(2,1)} async-done(((bf16[4,2,160,1024]{3,2,1,0:T(8,128)(2,1)}), bf16[1,2,160,1024]{3,2,1,0:T(8,128)(2,1)}) %reduce-scatter.7.cloned.1.call-update) | async-done | bytes 655376 | tf_op jit(solution)/shard_map/reduce_scatter | solution.py:457
  450.9 53.5 %reduce-scatter.9.cloned.1.call-done = bf16[1,2,160,1024]{3,2,1,0:T(8,128)(2,1)} async-done(((bf16[4,2,160,1024]{3,2,1,0:T(8,128)(2,1)}), bf16[1,2,160,1024]{3,2,1,0:T(8,128)(2,1)}) %reduce-scatter.9.cloned.1.call-update) | async-done | bytes 655376 | tf_op jit(solution)/shard_map/reduce_scatter | solution.py:457
  505.4 1.3 fusion.5
  508.1 1.9 fusion.3
  512.0 19.2 %all-gather.21.cloned.1.call-done = bf16[32,32,768]{2,1,0:T(8,128)(2,1)} async-done(((bf16[4,32,768]{2,1,0:T(8,128)(2,1)}), bf16[32,32,768]{2,1,0:T(8,128)(2,1)}) %all-gather.21.cloned.1.call-update) | async-done | bytes 1572880 | tf_op jit(solution)/shard_map/all_gather | solution.py:473
  531.2 5.6 reshape.441
  536.8 5.5 copy.59
  542.3 4.1 reshape.439
  546.4 5.0 fusion.33
  551.5 1.3 copy-done.12
  552.8 1.5 multiply_bitcast_fusion.2
  554.3 3.1 pad_maximum_fusion.2
  557.4 3.5 all-gather.25.cloned.1.call-done
  560.9 9.7 %fusion.35 = (f32[1,1024,1024]{2,1,0:T(8,128)}, f32[1024,1024]{1,0:T(8,128)S(1)}, f32[1024,1024]{1,0:T(8,128)}) fusion(f32[1024,1024]{1,0:T(8,128)} %param.28, f32[1024,1024]{1,0:T(8,128)} %param.33, bf16[1,1024,1024]{2,1,0:T(8,128)(2,1)} %all-gather.25.cloned.1.call-done), kind=kLoop, calls=%fused_computation.139 | loop fusion | flops 7340032 | bytes 23068672 | tf_op jit(solution)/shard_map/stack | solution.py:518
  570.6 7.1 %multiply_bitcast_fusion = f32[1,1024,1024]{2,1,0:T(8,128)S(1)} fusion(f32[1024,1024]{1,0:T(8,128)} %param.38, f32[1024,1024]{1,0:T(8,128)S(1)} %copy-done.1, f32[1024,1024]{1,0:T(8,128)} %get-tuple-element.75, f32[1024,1024]{1,0:T(8,128)S(1)} %get-tuple-element.74), kind=kLoop, calls=%fused_computation.4 | loop fusion | flops 6291456 | bytes 20971520 | tf_op jit(solution)/shard_map/stack | solution.py:518
  577.7 6.8 %pad_maximum_fusion.1 = f32[2,1024,1024]{2,1,0:T(8,128)} fusion(f32[1,1024,1024]{2,1,0:T(8,128)S(1)} %multiply_bitcast_fusion, f32[1,1024,1024]{2,1,0:T(8,128)} %get-tuple-element.73), kind=kLoop, calls=%fused_computation.1 | loop fusion | flops 2097152 | bytes 16777216 | tf_op jit(solution)/shard_map/stack | solution.py:518
  584.5 6.5 %all-gather.23.cloned.1.call-done = bf16[32,32,1024]{2,1,0:T(8,128)(2,1)} async-done(((bf16[4,32,1024]{2,1,0:T(8,128)(2,1)}), bf16[32,32,1024]{2,1,0:T(8,128)(2,1)}) %all-gather.23.cloned.1.call-update) | async-done | bytes 2097168 | tf_op jit(solution)/shard_map/all_gather | solution.py:472
  591.0 2.1 convert_bitcast_fusion
  593.1 2.7 copy.60
  595.9 4.1 copy.63
  599.9 7.1 %fusion.34 = (f32[1,256,4096]{2,1,0:T(8,128)}, f32[256,4096]{1,0:T(8,128)S(1)}) fusion(f32[256,4096]{1,0:T(8,128)S(1)} %copy-done.3, f32[256,4096]{1,0:T(8,128)S(1)} %bitcast.159, f32[256,4096]{1,0:T(8,128)} %param.32), kind=kLoop, calls=%fused_computation.138 | loop fusion | flops 6291456 | bytes 20971520 | tf_op jit(solution)/shard_map/stack | solution.py:518
  607.1 7.4 %multiply_bitcast_fusion.1 = f32[1,256,4096]{2,1,0:T(8,128)} fusion(f32[256,4096]{1,0:T(8,128)} %param.37, f32[256,4096]{1,0:T(8,128)S(1)} %copy-done.3, f32[256,4096]{1,0:T(8,128)S(1)} %bitcast.160, f32[256,4096]{1,0:T(8,128)S(1)} %get-tuple-element.77), kind=kLoop, calls=%fused_computation.7 | loop fusion | flops 6291456 | bytes 20971520 | tf_op jit(solution)/shard_map/stack | solution.py:518
  614.4 7.9 %pad_maximum_fusion = f32[2,256,4096]{2,1,0:T(8,128)} fusion(f32[1,256,4096]{2,1,0:T(8,128)} %multiply_bitcast_fusion.1, f32[1,256,4096]{2,1,0:T(8,128)} %get-tuple-element.76), kind=kLoop, calls=%fused_computation | loop fusion | flops 2097152 | bytes 16777216 | tf_op jit(solution)/shard_map/stack | solution.py:518
  (147 shorter events, 20.6 us)
Async XLA Ops:
  7.2 71.0 %all-gather.15.cloned.1.call-start = ((), (), s32[]{:S(2)}) async-start(), calls=%async_computation.15 | async-start | bytes 3276800 | tf_op jit(solution)/shard_map/all_gather | solution.py:447
  8.6 35.5 %copy-start.15 = (f32[3328]{0:T(1024)S(1)}, f32[3328]{0:T(1024)}, u32[]{:S(2)}) copy-start(f32[3328]{0:T(1024)} %param.29) | copy-start | bytes 39940
  9.5 49.0 %copy-start.22 = (s32[2,640]{1,0:T(2,128)S(1)}, s32[2,640]{1,0:T(2,128)}, u32[]{:S(2)}) copy-start(s32[2,640]{1,0:T(2,128)} %param.22) | copy-start | bytes 15364
  9.5 49.0 %copy-start.23 = (s32[2,640]{1,0:T(2,128)S(1)}, s32[2,640]{1,0:T(2,128)}, u32[]{:S(2)}) copy-start(s32[2,640]{1,0:T(2,128)} %param.23) | copy-start | bytes 15364
  9.5 49.7 %copy-start.9 = (f32[256,1024]{1,0:T(8,128)S(1)}, f32[256,1024]{1,0:T(8,128)}, u32[]{:S(2)}) copy-start(f32[256,1024]{1,0:T(8,128)} %param.26) | copy-start | bytes 3145732
  9.5 100.9 %all-gather.17.cloned.1.call-start = ((), (), s32[]{:S(2)}) async-start(), calls=%async_computation.16 | async-start | bytes 4128768 | tf_op jit(solution)/shard_map/all_gather | solution.py:425
  43.1 124.3 %all-gather.19.cloned.1.call-start = ((), (), s32[]{:S(2)}) async-start(), calls=%async_computation.17 | async-start | bytes 3276800 | tf_op jit(solution)/shard_map/all_gather | solution.py:447
  44.1 26.2 %copy-start.26 = (s32[2,1,13]{2,1,0:T(1,128)S(1)}, s32[2,1,13]{2,1,0:T(1,128)}, u32[]{:S(2)}) copy-start(s32[2,1,13]{2,1,0:T(1,128)} %param.24) | copy-start | bytes 316
  44.1 222.7 %reduce-scatter.11.cloned.1.call-start = ((), (), s32[]{:S(2)}) async-start(), calls=%async_computation.11 | async-start | bytes 1769472 | tf_op jit(solution)/shard_map/reduce_scatter | solution.py:467
  229.5 82.1 %reduce-scatter.17.cloned.1.call-start = ((), (), s32[]{:S(2)}) async-start(), calls=%async_computation.14 | async-start | bytes 2359296 | tf_op jit(solution)/shard_map/reduce_scatter | solution.py:462
  230.1 123.9 %reduce-scatter.13.cloned.1.call-start = ((), (), s32[]{:S(2)}) async-start(), calls=%async_computation.12 | async-start | bytes 589824 | tf_op jit(solution)/shard_map/reduce_scatter | solution.py:464
  230.7 81.0 %copy-start.6 = (bf16[2,160,1024]{2,1,0:T(8,128)(2,1)S(1)}, bf16[2,160,1024]{2,1,0:T(8,128)(2,1)}, u32[]{:S(2)}) copy-start(bf16[2,160,1024]{2,1,0:T(8,128)(2,1)} %param.20) | copy-start | bytes 1966084
  230.7 163.7 %reduce-scatter.15.cloned.1.call-start = ((), (), s32[]{:S(2)}) async-start(), calls=%async_computation.13 | async-start | bytes 2359296 | tf_op jit(solution)/shard_map/reduce_scatter | solution.py:466
  230.7 81.3 %copy-start.25 = (f32[1,768]{1,0:T(1,128)S(1)}, f32[1,768]{1,0:T(1,128)}, u32[]{:S(2)}) copy-start(f32[1,768]{1,0:T(1,128)} %get-tuple-element.59) | copy-start | bytes 9220
  230.7 81.5 %copy-start.24 = (f32[1,1024]{1,0:T(1,128)S(1)}, f32[1,1024]{1,0:T(1,128)}, u32[]{:S(2)}) copy-start(f32[1,1024]{1,0:T(1,128)} %get-tuple-element.60) | copy-start | bytes 12292
  230.7 81.8 %copy-start.16 = (f32[8,1024]{1,0:T(8,128)S(1)}, f32[8,1024]{1,0:T(8,128)}, u32[]{:S(2)}) copy-start(f32[8,1024]{1,0:T(8,128)} %get-tuple-element.57) | copy-start | bytes 98308
  230.8 81.8 %copy-start.17 = (f32[8,1024]{1,0:T(8,128)S(1)}, f32[8,1024]{1,0:T(8,128)}, u32[]{:S(2)}) copy-start(f32[8,1024]{1,0:T(8,128)} %get-tuple-element.58) | copy-start | bytes 98308
  230.8 81.8 %copy-start.18 = (f32[8,1024]{1,0:T(8,128)S(1)}, f32[8,1024]{1,0:T(8,128)}, u32[]{:S(2)}) copy-start(f32[8,1024]{1,0:T(8,128)} %get-tuple-element.55) | copy-start | bytes 98308
  230.8 81.8 %copy-start.19 = (f32[8,1024]{1,0:T(8,128)S(1)}, f32[8,1024]{1,0:T(8,128)}, u32[]{:S(2)}) copy-start(f32[8,1024]{1,0:T(8,128)} %get-tuple-element.56) | copy-start | bytes 98308
  231.4 121.2 %copy-start.20 = (f32[3328]{0:T(1024)S(1)}, f32[3328]{0:T(1024)}, u32[]{:S(2)}) copy-start(f32[3328]{0:T(1024)} %param.39) | copy-start | bytes 39940
  231.4 121.2 %copy-start.21 = (f32[3328]{0:T(1024)S(1)}, f32[3328]{0:T(1024)}, u32[]{:S(2)}) copy-start(f32[3328]{0:T(1024)} %param.34) | copy-start | bytes 39940
  231.4 218.3 %reduce-scatter.7.cloned.1.call-start = ((), (), s32[]{:S(2)}) async-start(), calls=%async_computation.9 | async-start | bytes 3276800 | tf_op jit(solution)/shard_map/reduce_scatter | solution.py:457
  232.2 272.1 %reduce-scatter.9.cloned.1.call-start = ((), (), s32[]{:S(2)}) async-start(), calls=%async_computation.10 | async-start | bytes 3276800 | tf_op jit(solution)/shard_map/reduce_scatter | solution.py:457
  232.9 298.3 %all-gather.21.cloned.1.call-start = ((), (), s32[]{:S(2)}) async-start(), calls=%async_computation.18 | async-start | bytes 1769472 | tf_op jit(solution)/shard_map/all_gather | solution.py:473
  278.9 282.0 %all-gather.25.cloned.1.call-start = ((), (), s32[]{:S(2)}) async-start(), calls=%async_computation.20 | async-start | bytes 2359296 | tf_op jit(solution)/shard_map/all_gather | solution.py:470
  367.9 34.8 %copy-start.10 = (f32[256,1024]{1,0:T(8,128)}, f32[256,1024]{1,0:T(8,128)S(1)}, u32[]{:S(2)}) copy-start(f32[256,1024]{1,0:T(8,128)S(1)} %get-tuple-element.79) | copy-start | bytes 3145732
  394.4 18.4 %all-to-all-start.2 = ((bf16[4,32,1024]{2,1,0:T(8,128)(2,1)}), bf16[4,32,1024]{2,1,0:T(8,128)(2,1)S(1)}, u32[]{:S(2)}, u32[]{:S(2)}) async-start(bf16[4,32,1024]{2,1,0:T(8,128)(2,1)} %bitcast.170), calls=%async_computation.7 | async-start | bytes 524288 | tf_op jit(solution)/shard_map/all_to_all | solution.py:468
  399.0 192.1 %all-gather.23.cloned.1.call-start = ((), (), s32[]{:S(2)}) async-start(), calls=%async_computation.19 | async-start | bytes 2359296 | tf_op jit(solution)/shard_map/all_gather | solution.py:472
  399.1 2.1 copy-start.11
  401.2 106.9 %copy-start.13 = (bf16[2,160,1024]{2,1,0:T(8,128)(2,1)S(1)}, bf16[2,160,1024]{2,1,0:T(8,128)(2,1)}, u32[]{:S(2)}) copy-start(bf16[2,160,1024]{2,1,0:T(8,128)(2,1)} %param.21) | copy-start | bytes 1966084
  412.8 0.7 copy-start.14
  546.4 5.0 copy-start.2
  546.4 5.0 copy-start.7
  546.4 6.4 %copy-start.12 = (f32[256,3072]{1,0:T(8,128)S(1)}, f32[256,3072]{1,0:T(8,128)}, u32[]{:S(2)}) copy-start(f32[256,3072]{1,0:T(8,128)} %param.35) | copy-start | bytes 9437188
  551.4 2.9 copy-start.8
  560.9 9.7 %copy-start.1 = (f32[1024,1024]{1,0:T(8,128)S(1)}, f32[1024,1024]{1,0:T(8,128)}, u32[]{:S(2)}) copy-start(f32[1024,1024]{1,0:T(8,128)} %param.28) | copy-start | bytes 12582916
  570.6 7.1 %copy-start.5 = (f32[1024,1024]{1,0:T(8,128)}, f32[1024,1024]{1,0:T(8,128)S(1)}, u32[]{:S(2)}) copy-start(f32[1024,1024]{1,0:T(8,128)S(1)} %get-tuple-element.74) | copy-start | bytes 12582916
  595.8 4.1 copy-start.3
  599.9 7.1 %copy-start = (f32[32,8,4,1024]{3,1,2,0:T(8,128)}, f32[32,8,4,1024]{3,1,2,0:T(8,128)S(1)}, u32[]{:S(2)}) copy-start(f32[32,8,4,1024]{3,1,2,0:T(8,128)S(1)} %copy.63) | copy-start | bytes 12582916
  607.1 7.4 %copy-start.4 = (f32[256,4096]{1,0:T(8,128)}, f32[256,4096]{1,0:T(8,128)S(1)}, u32[]{:S(2)}) copy-start(f32[256,4096]{1,0:T(8,128)S(1)} %get-tuple-element.77) | copy-start | bytes 12582916
Sparse Core Ops, SparseCore 0:
  10.1 64.7 all-gather.14
  76.9 33.5 all-gather.16
  112.6 54.7 all-gather.18
  229.6 37.0 reduce-scatter.10
  270.4 41.1 reduce-scatter.16
  315.1 34.2 reduce-scatter.12
  353.2 41.1 reduce-scatter.14
  397.2 52.4 reduce-scatter.6
  452.6 51.6 reduce-scatter.8
  506.1 25.1 all-gather.20
  533.1 27.7 all-gather.24
  563.2 27.7 all-gather.22
